TPU v7x, 128 devices: a whole 4x4x4 slice. The times are simulated.
128 devices in a mesh: sample: 8 (over z_lo, x), depth: 16 (over z_hi, y, core).
Axes of the slice: x: 4, y: 4, z: 4 (z_hi: 2, z_lo: 2; z = z_hi * 2 + z_lo), core: 2. Of those that a mesh axis runs over, the one named last changes fastest.
Arguments:
- volume: bfloat16 [8, 16, 32, 2048], P('sample', 'depth'), may hold values from -6 to 6
- conv1_weight: bfloat16 [27, 64, 64], replicated, may hold values from -0.15625 to 0.15625
- conv2_weight: bfloat16 [27, 1024, 1024], P(None, 'depth'), may hold values from -0.0390625 to 0.0390625
- cotangent: bfloat16 [8, 16, 8, 8, 1024], P('sample', 'depth'), may hold values from -6 to 6
Outputs:
- features_out: bfloat16 [8, 16, 8, 8, 1024], P('sample', 'depth')
- grad_volume: bfloat16 [8, 16, 32, 2048], P('sample', 'depth')
- grad_conv1: float32 [27, 64, 64], replicated
- grad_conv2: float32 [27, 1024, 1024], P(None, 'depth')
All inputs are finite; a program needn't handle non-finite values.
Results may differ from a plain program's by a relative error of at most 0.014.
Values may be sent and summed in bfloat16 or wider, within the bound.
A program may use at most 256 MiB of HBM per device.

v0:
```python
import functools
import math

import jax
import jax.numpy as jnp
from jax import lax
from jax.experimental import pallas as pl
from jax.experimental.pallas import tpu as pltpu
from jax.sharding import PartitionSpec as P

MESH = pl.DeviceIdType.MESH
F32 = jnp.float32
BF16 = jnp.bfloat16
ROOT = 0.7978845608028654
CUBIC = 0.044715
SCALE1 = 1.0 / math.sqrt(8 * 16 * 32 * 32)
SCALE2 = 1.0 / math.sqrt(8 * 16 * 8 * 8)
VM = pl.BlockSpec(memory_space=pltpu.VMEM)
ANY = pl.BlockSpec(memory_space=pl.ANY)
LIMIT = 60 * 1024 * 1024


def where_am_i():
    s = lax.axis_index("sample")
    d = lax.axis_index("depth")
    return s, d


def rcopy(src, dst, ss, rs, dev):
    return pltpu.make_async_remote_copy(
        src_ref=src, dst_ref=dst, send_sem=ss, recv_sem=rs, device_id=dev, device_id_type=MESH
    )


def depth_peer(d, jz, jy, jc):
    zh, y, c = d // 8, (d // 2) % 4, d % 2
    return ((zh + jz) % 2) * 8 + ((y + jy) % 4) * 2 + (c + jc) % 2


def depth_src(d, jz, jy, jc):
    zh, y, c = d // 8, (d // 2) % 4, d % 2
    return ((zh + jz) % 2) * 8 + ((y + 4 - jy) % 4) * 2 + (c + jc) % 2


def sample_peer(s, jz, jx):
    return ((s // 4 + jz) % 2) * 4 + (s % 4 + jx) % 4


def sample_src(s, jz, jx):
    return ((s // 4 + jz) % 2) * 4 + (s % 4 + 4 - jx) % 4


CHIPS = [(jz, jy) for jz in range(2) for jy in range(4) if (jz, jy) != (0, 0)]
SAMPS = [(jz, jx) for jz in range(2) for jx in range(4) if (jz, jx) != (0, 0)]


def barrier(devs):
    bar = pltpu.get_barrier_semaphore()
    for dev in devs:
        pl.semaphore_signal(bar, inc=1, device_id=dev, device_id_type=MESH)
    pl.semaphore_wait(bar, len(devs))


def onehot(shape, fn):
    row = lax.broadcasted_iota(jnp.int32, shape, 0)
    col = lax.broadcasted_iota(jnp.int32, shape, 1)
    return jnp.where(fn(row, col), 1.0, 0.0).astype(BF16)


def dot(a, b):
    return jnp.dot(a, b, preferred_element_type=F32)


def nat(rho):
    return 4 * (rho % 8) + rho // 8


def call(kern, outs, ins, scratch, name, cid=None, specs=None, out_specs=None, **kw):
    params = dict(vmem_limit_bytes=LIMIT)
    if cid is not None:
        params.update(collective_id=cid, has_side_effects=True)
    return pl.pallas_call(
        kern,
        out_shape=outs,
        in_specs=specs or [VM] * len(ins),
        out_specs=out_specs or [VM] * len(outs),
        scratch_shapes=scratch,
        compiler_params=pltpu.CompilerParams(**params),
        name=name,
    )(*ins)


def sds(shape, dtype=BF16):
    return jax.ShapeDtypeStruct(shape, dtype)


def depth_of(zh, y, c):
    return zh * 8 + y * 2 + c


def fill_rows(lhs, planes, perms):
    zero = jnp.zeros((32, 128), BF16)
    for a in range(3):
        for b in range(3):
            x = planes[a] if perms[b] is None else dot(perms[b], planes[a]).astype(BF16)
            xp = jnp.concatenate([zero, x, zero], axis=1)
            for j in range(8):
                lhs[pl.ds(j * 32, 32), pl.ds((3 * a + b) * 512, 512)] = xp[:, 256 * j : 256 * j + 512]


def edge_planes(prev, own, nxt, d):
    zero = jnp.zeros_like(own)
    return [jnp.where(d > 0, prev, zero), own, jnp.where(d < 15, nxt, zero)]


def gelu_parts(value):
    inner = ROOT * (value + CUBIC * value * value * value)
    return jnp.tanh(inner)


def row_shift(x, b):
    if b == 1:
        return x
    rows = x.shape[0]
    lane = lax.broadcasted_iota(jnp.int32, x.shape, 0) % 8
    if b == 0:
        return jnp.where(lane == 0, 0.0, pltpu.roll(x, 1, 0))
    return jnp.where(lane == 7, 0.0, pltpu.roll(x, rows - 1, 0))


def col_shift(x, c):
    if c == 1:
        return x
    zero = jnp.zeros((x.shape[0], 8, x.shape[2]), x.dtype)
    if c == 0:
        return jnp.concatenate([zero, x[:, :56]], axis=1)
    return jnp.concatenate([x[:, 8:], zero], axis=1)


def taps10(x, s2):
    n = x.shape[0]
    flat = x.astype(F32).reshape(n * 64, 128)
    for b in range(3):
        y = row_shift(flat, b).reshape(n, 64, 128)
        for c in range(3):
            s2[:, :, (3 * b + c) * 128 : (3 * b + c + 1) * 128] = col_shift(y, c).astype(BF16)


def put_band(band, ab, w3):
    zero = jnp.zeros((64, 64), BF16)
    left = jnp.concatenate([w3, zero], axis=0)
    right = jnp.concatenate([zero, w3], axis=0)
    both = jnp.concatenate([left, right], axis=1)
    band[pl.ds(ab * 512 + 64, 256), 0:128] = both
    band[pl.ds(ab * 512 + 192, 256), 128:256] = both


def fill_band(band, w1):
    band[...] = jnp.zeros_like(band)
    for ab in range(9):
        put_band(band, ab, w1[3 * ab : 3 * ab + 3].reshape(192, 64))


def fill_band_back(band, w1):
    band[...] = jnp.zeros_like(band)
    for ab in range(9):
        top = 3 * (8 - ab) + 2
        w3 = [jnp.transpose(w1[top - c].astype(F32)).astype(BF16) for c in range(3)]
        put_band(band, ab, jnp.concatenate(w3, axis=0))


CHUNKS = [(4 * q, min(4, 27 - 4 * q)) for q in range(7)]
XF = (0, 1, 2)
ZF = (3, 4, 5, 6)


def mega_kernel(
    v, cot, w1, w,
    feat, gvol, tout, gw,
    vp, vn, cotp, mine, cb, csl, wv, mk, moved, lhs, lhsb, band, bandb, s2o, s2, part, frecv,
    gm, grecv, acc, wacc, pre, ownf, psend, precv, gpn, gp, gn, tbuf, pbuf, pbuf2, own, rbuf, dbuf, rbuf2,
    wsem, hsem, asem, csem, xsem, msem, ssem, gsem, rsem, psem, nsend, nrecv, ksem, tsem,
):
    s, d = where_am_i()
    zh, y, c = d // 8, (d // 2) % 4, d % 2
    m = d // 2
    zl = s // 4
    up, down = (d + 1) % 16, (d + 15) % 16
    partner = depth_of(zh, y, 1 - c)
    wl = pltpu.make_async_copy(w, wv.at[:, c], wsem.at[0])
    wl.start()
    barrier(
        [(s, depth_peer(d, jz, jy, jc)) for jz in range(2) for jy in range(4) for jc in range(2) if (jz, jy, jc) != (0, 0, 0)]
        + [(sample_peer(s, jz, jx), d) for jz, jx in SAMPS]
    )
    late = []

    def spread(src_of, dst, sems, edge):
        k = d % 8
        for i, (jz, jy) in enumerate([(0, 0)] + CHIPS):
            t = depth_of((zh + jz) % 2, (y + jy) % 4, zh)
            cp = rcopy(src_of(t // 2), dst(k + edge), sems.at[i], sems.at[16 + k], (s, t))
            if i:
                cp.start()
                late.append((None, cp))
            else:

                @pl.when(t != d)
                def _(cp=cp):
                    cp.start()

                late.append((t != d, cp))
        if edge:
            rim = (d == 7) | (d == 8)
            for i, (jz, jy) in enumerate(CHIPS):
                t = depth_of((zh + jz) % 2, (y + jy) % 4, 1 - zh)
                cp = rcopy(src_of(t // 2), dst(zh * 9), sems.at[8 + i], sems.at[24], (s, t))

                @pl.when(rim)
                def _(cp=cp):
                    cp.start()

                late.append((rim, cp))

    def spread_local(value, dst_ref, edge):
        @pl.when(c == zh)
        def _():
            dst_ref(d % 8 + edge, value)

        if edge:

            @pl.when((d == 7) | (d == 8))
            def _():
                dst_ref(zh * 9, value)

    def spread_wait(dst, sems, edge):
        for k in range(8):

            @pl.when(8 * c + k != d)
            def _(k=k):
                rcopy(dst(k + edge), dst(k + edge), sems.at[0], sems.at[16 + k], (s, partner)).wait_recv()

        if edge:
            q = 9 - 9 * c

            @pl.when(8 - c != d)
            def _():
                rcopy(dst(q), dst(q), sems.at[0], sems.at[24], (s, partner)).wait_recv()

    def to_owner(src, dst, sems, lo=0):
        for i in range(8):
            p = 8 * c + i
            cp = rcopy(src.at[i], dst.at[m], sems.at[i], sems.at[8 + m], (s, p))

            @pl.when(p != d)
            def _(cp=cp):
                cp.start()

            @pl.when(p == d)
            def _(i=i):
                dst[m] = src[i]

            late.append((p != d, cp))

    def owner_wait(dst, sems):
        for j in range(8):

            @pl.when(2 * j + zh != d)
            def _(j=j):
                rcopy(dst.at[j], dst.at[j], sems.at[0], sems.at[8 + j], (s, partner)).wait_recv()

    halo = [rcopy(v, vp, hsem.at[0], hsem.at[1], (s, up)), rcopy(v, vn, hsem.at[2], hsem.at[3], (s, down))]
    for h in halo:
        h.start()
    wx = rcopy(w, wv.at[:, c], wsem.at[1], wsem.at[2], (s, partner))
    wx.start()
    perm64 = onehot((64, 64), lambda u, q: q == (u % 8) * 8 + u // 8)
    cotp[...] = dot(perm64, cot[...]).astype(BF16)
    for i, (jz, jx) in enumerate(SAMPS):
        t = sample_peer(s, jz, jx)
        cp = rcopy(cotp.at[:, pl.ds(pl.multiple_of(t * 128, 128), 128)], mine.at[s], asem.at[i], asem.at[7 + i], (t, d))
        cp.start()
        late.append((None, cp))
    spread(lambda t: cotp, lambda k: cb.at[k], csem, 1)

    def put_cb(k, value):
        cb[k] = value

    spread_local(cotp[...], put_cb, 1)
    mine[s] = cotp[:, pl.ds(pl.multiple_of(s * 128, 128), 128)]
    cb[9 * c] = jnp.zeros((64, 1024), BF16)
    mk[:, 9 * c] = jnp.zeros((8, 64, 128), BF16)

    fill_band(band, w1)
    perms = [onehot((32, 32), lambda rho, i, b=b: i == nat(rho) + b - 1) for b in range(3)]
    for h in halo:
        h.wait()
    fill_rows(lhs, edge_planes(vp[...], v[...], vn[...], d), perms)
    res = dot(lhs[...], band[...])
    for r in range(4):
        z = jnp.concatenate([res[j * 32 + r * 8 : j * 32 + r * 8 + 8] for j in range(8)], axis=0)
        pre[r] = z
        hid = (0.5 * z * (1.0 + gelu_parts(z))).astype(BF16)
        moved[2 * r] = hid[:, 0:128]
        moved[2 * r + 1] = hid[:, 128:256]
    spread(lambda t: moved.at[t], lambda k: mk.at[s, k], msem, 1)

    def put_mk(k, value):
        mk[s, k] = value

    spread_local(moved[m], put_mk, 1)

    for i, (jz, jx) in enumerate(SAMPS):
        t = sample_src(s, jz, jx)
        rcopy(mine.at[t], mine.at[t], asem.at[i], asem.at[7 + i], (t, d)).wait_recv()
    spread(lambda t: mine, lambda k: csl.at[k], xsem, 0)

    def put_csl(k, value):
        csl[k] = value

    spread_local(mine[...], put_csl, 0)
    fill_band_back(bandb, w1)
    wacc[...] = jnp.zeros_like(wacc)

    spread_wait(lambda k: mk.at[s, k], msem, 1)
    nine = pl.ds(1 - c, 9)
    for i in range(1, 8):
        cp = rcopy(mk.at[s, nine], mk.at[s, nine], ssem.at[i - 1], ssem.at[6 + i], (sample_peer(s, i // 4, i % 4), d))
        cp.start()
        late.append((None, cp))
    taps10(mk[s], s2o)

    wl.wait()
    wx.wait()
    spread_wait(lambda k: cb.at[k], csem, 1)

    def back(i, _):
        tot = jnp.zeros((512, 384), F32)
        for a in range(3):
            rows = cb[2 - a : 10 - a].reshape(512, 1024)
            wt = wv[pl.ds(9 * a + 3 * i, 3)].reshape(384, 1024)
            tot = tot + lax.dot_general(rows, wt, (((1,), (1,)), ((), ())), preferred_element_type=F32)
        for j in range(3):
            acc[3 * i + j] = tot[:, 128 * j : 128 * j + 128]
        return 0

    lax.fori_loop(0, 3, back, 0)
    total = jnp.zeros((8, 64, 128), F32)
    for b in range(3):
        inner = jnp.zeros((8, 64, 128), F32)
        for cc in range(3):
            inner = inner + col_shift(acc[3 * b + cc].reshape(8, 64, 128), 2 - cc)
        total = total + row_shift(inner.reshape(512, 128), 2 - b).reshape(8, 64, 128)
    gm[...] = total.astype(BF16)
    to_owner(gm, grecv, gsem)

    spread_wait(lambda k: csl.at[k], xsem, 0)

    def wpart(t, ref):
        ct = jnp.transpose(csl[:, t].reshape(512, 128).astype(F32)).astype(BF16)
        for a in range(3):
            wacc[:, 1152 * a : 1152 * a + 1152] += dot(ct, ref[a : a + 8].reshape(512, 1152))

    wpart(s, s2o)

    def wgrad(i, _):
        t = ((zl + i // 4) % 2) * 4 + (s % 4 + 4 - i % 4) % 4
        rcopy(mk.at[t, nine], mk.at[t, nine], ssem.at[i - 1], ssem.at[6 + i], (s, partner)).wait_recv()
        taps10(mk[t], s2)
        wpart(t, s2)
        return 0

    lax.fori_loop(1, 8, wgrad, 0)

    pcp = []
    for q, (lo, n) in enumerate(CHUNKS):
        for t in range(lo, lo + n):
            x = jnp.transpose(wacc[:, t * 128 : t * 128 + 128] * SCALE2)
            ownf[t] = jnp.where(c == 0, x[0:64], x[64:128])
            psend[t] = jnp.where(c == 0, x[64:128], x[0:64]).astype(BF16)
        cp = rcopy(psend.at[pl.ds(lo, n)], precv.at[pl.ds(lo, n)], psem.at[q], psem.at[7 + q], (s, partner))
        cp.start()
        pcp.append(cp)

    xp, xm, zo = sample_peer(s, 0, 1), sample_peer(s, 0, 3), sample_peer(s, 1, 0)
    x2 = sample_peer(s, 0, 2)
    oxp, oxm, ox2 = sample_peer(s, 1, 1), sample_peer(s, 1, 3), sample_peer(s, 1, 2)

    def nsem(q, kind):
        return nsend.at[7 * q + kind], nrecv.at[7 * q + kind]

    def send(q, kind, block, dev):
        ref = gw.at[block, pl.ds(*CHUNKS[q])]
        cp = rcopy(ref, ref, *nsem(q, kind), (dev, d))
        cp.start()
        late.append((None, cp))

    def recv(q, kind, block):
        ref = gw.at[block, pl.ds(*CHUNKS[q])]
        rcopy(ref, ref, *nsem(q, kind), (s, partner)).wait_recv()

    for q, (lo, n) in enumerate(CHUNKS):
        pcp[q].wait()
        gw[s, pl.ds(lo, n)] = (ownf[pl.ds(lo, n)] + precv[pl.ds(lo, n)].astype(F32)).astype(BF16)
        if q in ZF:
            send(q, 0, s, zo)
        send(q, 1, s, xp)
        send(q, 2, s, xm)
    for q in XF:
        send(q, 0, s, zo)

    owner_wait(grecv, gsem)
    gpf = []
    for r in range(4):
        z = pre[r]
        th = gelu_parts(z)
        slope = 0.5 * (1.0 + th) + 0.5 * z * (1.0 - th * th) * ROOT * (1.0 + 3.0 * CUBIC * z * z)
        gpf.append(jnp.concatenate([grecv[2 * r], grecv[2 * r + 1]], axis=1).astype(F32) * slope)
    for j in range(8):
        rows = jnp.concatenate([gpf[r][8 * j : 8 * j + 8] for r in range(4)], axis=0)
        gpn[:, 256 * j : 256 * j + 256] = rows.astype(BF16)
    ghalo = [rcopy(gpn, gp, hsem.at[4], hsem.at[5], (s, up)), rcopy(gpn, gn, hsem.at[6], hsem.at[7], (s, down))]
    for h in ghalo:
        h.start()

    gx = jnp.concatenate([gpn[:, 256 * j : 256 * j + 256] for j in range(8)], axis=0)
    gt = jnp.transpose(gx.astype(F32)).astype(BF16)
    for ab in range(9):
        o = dot(gt, lhs[:, 512 * ab : 512 * ab + 512])
        even = o[0:64, 0:256] + o[128:192, 128:384]
        t = o[64:128, 128:384] + o[192:256, 256:512] + pltpu.roll(even, 192, 1)
        tbuf[64 * ab : 64 * ab + 64] = (t * SCALE1).astype(BF16)
    tbuf[576:640] = jnp.zeros((64, 256), BF16)
    lane = pl.ds(pl.multiple_of(c * 128, 128), 128)
    lane2 = pl.ds(pl.multiple_of(128 - c * 128, 128), 128)
    k1 = rcopy(tbuf.at[:, lane2], pbuf, ksem.at[0], ksem.at[1], (s, partner))
    k1.start()

    for q in XF:
        recv(q, 1, xm)
        if q % 2 == 0:
            send(q, 3, xm, xp)
        send(q, 4, xm, zo)
        recv(q, 2, xp)
        if q % 2:
            send(q, 3, xp, xm)
        send(q, 5, xp, zo)

    k1.wait()
    own[...] = (tbuf[:, lane].astype(F32) + pbuf[...].astype(F32)).astype(BF16)
    k2s = []
    for i, (jz, jy) in enumerate(CHIPS):
        t = depth_peer(d, jz, jy, 0)
        k2s.append(rcopy(own.at[pl.ds(pl.multiple_of((t // 2) * 80, 16), 80)], rbuf.at[i], tsem.at[i], tsem.at[7 + i], (s, t)))
        k2s[-1].start()

    for q in ZF:
        recv(q, 0, zo)
        send(q, 4, zo, xp)
        send(q, 5, zo, xm)

    def fwd(i, _):
        tot = jnp.zeros((256, 1024), F32)
        for a in range(3):
            tot = tot + dot(s2o[pl.ds(4 * i + a, 4)].reshape(256, 1152), wv[9 * a : 9 * a + 9].reshape(1152, 1024))
        part[pl.ds(4 * i, 4)] = tot.astype(BF16).reshape(4, 64, 1024)
        return 0

    lax.fori_loop(0, 2, fwd, 0)
    to_owner(part, frecv, rsem)

    for q in ZF:
        recv(q, 1, xm)
        if q % 2 == 0:
            send(q, 3, xm, xp)
        recv(q, 2, xp)
        if q % 2:
            send(q, 3, xp, xm)
    for q in XF:
        recv(q, 3, x2)
        send(q, 6, x2, zo)

    piece = pl.ds(pl.multiple_of(m * 80, 16), 80)
    tot = own[piece].astype(F32)
    for i in range(7):
        k2s[i].wait()
        tot = tot + rbuf[i].astype(F32)
    dbuf[7] = tot.astype(BF16)
    k3s = []
    for i, (jz, jx) in enumerate(SAMPS):
        k3s.append(rcopy(dbuf.at[7], dbuf.at[i], tsem.at[14 + i], tsem.at[21 + i], (sample_peer(s, jz, jx), d)))
        k3s[-1].start()

    for h in ghalo:
        h.wait()
    perms = [onehot((32, 32), lambda u, q, b=b: nat(q) == nat(u) + b - 1) for b in range(3)]
    perms[1] = None
    fill_rows(lhsb, edge_planes(gp[...], gpn[...], gn[...], d), perms)
    res = dot(lhsb[...], bandb[...]).astype(BF16)
    wide = jnp.concatenate([res[32 * j : 32 * j + 32] for j in range(8)], axis=1)
    gvol[...] = dot(onehot((32, 32), lambda i, q: nat(q) == i), wide).astype(BF16)

    for q in ZF:
        recv(q, 4, oxm)
        if q % 2 == 0:
            send(q, 6, oxm, xp)
        recv(q, 5, oxp)
        if q % 2:
            send(q, 6, oxp, xm)

    for x in k3s:
        x.wait()
    tot = None
    for j in range(8):
        idx = ((j // 4 + zl) % 2) * 4 + (s % 4 + 4 - j % 4) % 4
        idx = jnp.where(idx == 0, 7, idx - 1)
        val = dbuf[idx].astype(F32)
        tot = val if tot is None else tot + val
    own[piece] = tot.astype(BF16)
    k4s = []
    for i, (jz, jy) in enumerate(CHIPS):
        k4s.append(rcopy(own.at[piece], rbuf2.at[i], tsem.at[28 + i], tsem.at[35 + i], (s, depth_peer(d, jz, jy, 0))))
        k4s[-1].start()

    owner_wait(frecv, rsem)
    tot = frecv[0].astype(F32)
    for i in range(1, 8):
        tot = tot + frecv[i].astype(F32)
    feat[...] = dot(perm64, tot.astype(BF16)).astype(BF16)

    for i, (jz, jy) in enumerate(CHIPS):
        k4s[i].wait()
        own[pl.ds(pl.multiple_of((depth_src(d, jz, jy, 0) // 2) * 80, 16), 80)] = rbuf2[i]
    k5 = rcopy(own, pbuf2, ksem.at[2], ksem.at[3], (s, partner))
    k5.start()
    tout[:, lane] = own[...]
    k5.wait()
    tout[:, lane2] = pbuf2[...]

    for q in XF:
        recv(q, 0, zo)
        recv(q, 4, oxm)
        recv(q, 5, oxp)
        recv(q, 6, ox2)
    for q in ZF:
        recv(q, 3, x2)
        recv(q, 6, ox2)
    for cond, cp in late:
        if cond is None:
            cp.wait_send()
        else:

            @pl.when(cond)
            def _(cp=cp):
                cp.wait_send()


def mega(v, cot, w1, w):
    dma = pltpu.SemaphoreType.DMA
    vm = lambda *shape: pltpu.VMEM(shape, BF16)
    vf = lambda *shape: pltpu.VMEM(shape, F32)
    scratch = [
        vm(32, 2048), vm(32, 2048), vm(64, 1024), vm(8, 64, 128), vm(10, 64, 1024), vm(8, 8, 64, 128),
        vm(27, 2, 64, 1024), vm(8, 10, 64, 128), vm(8, 64, 128), vm(256, 4608), vm(256, 4608), vm(4608, 256),
        vm(4608, 256), vm(10, 64, 1152), vm(10, 64, 1152), vm(8, 64, 1024), vm(8, 64, 1024),
        vm(8, 64, 128), vm(8, 64, 128), vf(9, 512, 128), vf(128, 3456), vf(4, 64, 256), vf(27, 64, 128),
        vm(27, 64, 128), vm(27, 64, 128), vm(32, 2048), vm(32, 2048), vm(32, 2048), vm(640, 256), vm(640, 128),
        vm(640, 128), vm(640, 128), vm(7, 80, 128), vm(8, 80, 128), vm(7, 80, 128),
        dma((3,)), dma((8,)), dma((14,)), dma((25,)), dma((25,)), dma((25,)), dma((14,)), dma((16,)), dma((16,)),
        dma((14,)), dma((49,)), dma((49,)), dma((4,)), dma((42,)),
    ]
    return pl.pallas_call(
        mega_kernel,
        out_shape=[sds((64, 1024)), sds((32, 2048)), sds((640, 256)), sds((8, 27, 64, 128))],
        in_specs=[VM, VM, VM, ANY],
        out_specs=[VM] * 4,
        scratch_shapes=scratch,
        compiler_params=pltpu.CompilerParams(vmem_limit_bytes=LIMIT, collective_id=1, has_side_effects=True),
        name="step",
    )(v, cot, w1, w)


def finish_kernel(gw, t, f, g, o2, o1, of, og):
    for q in range(8):
        o2[:, :, 128 * q : 128 * q + 128] = gw[q].astype(F32)

    @pl.when(pl.program_id(0) == 0)
    def _():
        of[...] = f[...]
        og[...] = g[...]
        for ab in range(9):
            x = jnp.transpose(t[64 * ab : 64 * ab + 64].astype(F32))
            o1[3 * ab : 3 * ab + 3] = x[0:192].reshape(3, 64, 64)


def finish(gw, t, f, g):
    whole = lambda *shape: pl.BlockSpec(shape, lambda i: (0,) * len(shape))
    return pl.pallas_call(
        finish_kernel,
        grid=(9,),
        out_shape=[sds((27, 64, 1024), F32), sds((27, 64, 64), F32), sds((64, 1024)), sds((32, 2048))],
        in_specs=[pl.BlockSpec((8, 3, 64, 128), lambda i: (0, i, 0, 0)), whole(640, 256), whole(64, 1024), whole(32, 2048)],
        out_specs=[pl.BlockSpec((3, 64, 1024), lambda i: (i, 0, 0)), whole(27, 64, 64), whole(64, 1024), whole(32, 2048)],
        compiler_params=pltpu.CompilerParams(vmem_limit_bytes=LIMIT),
        name="finish",
    )(gw, t, f, g)


def on_device(volume, conv1_weight, conv2_weight, cotangent):
    feat, gvol, tall, gw = mega(volume.reshape(32, 2048), cotangent.reshape(64, 1024), conv1_weight, conv2_weight)
    o2, o1, feat, gvol = finish(gw, tall, feat, gvol)
    return feat.reshape(1, 1, 8, 8, 1024), gvol.reshape(1, 1, 32, 2048), o1, o2


def solution(mesh):
    return jax.shard_map(
        on_device,
        mesh=mesh,
        in_specs=(P("sample", "depth", None, None), P(), P(None, "depth", None), P("sample", "depth", None, None, None)),
        out_specs=(P("sample", "depth", None, None, None), P("sample", "depth", None, None), P(), P(None, "depth", None)),
        check_vma=False,
    )
```

profile of v0, /device:TPU:1, one launch (start us, length us, event | category | flops | bytes accessed | tf_op | source)
XLA Modules:
  0.0 121.7 jit_solution(2298725514497477195)
XLA Ops:
  0.6 112.7 %step.1 = (bf16[64,1024]{1,0:T(8,128)(2,1)}, bf16[32,2048]{1,0:T(8,128)(2,1)}, bf16[640,256]{1,0:T(8,128)(2,1)}, bf16[8,27,64,128]{3,2,1,0:T(8,128)(2,1)}) custom-call(bf16[32,2048]{1,0:T(8,128)(2,1)} %bitcast.4, bf16[64,1024]{1,0:T(8,128)(2,1)} %bitcast.5, bf16[27,64,64]{2,1,0:T(8,128)(2,1)} %w1.1, bf16[27,64,1024]{2,1,0:T(8,128)(2,1)} %w.1), custom_call_target="tpu_custom_call" | custom-call | tf_op jit(solution)/shard_map/step/pallas_call | solution.py:572
  113.4 8.4 %finish.1 = (f32[27,64,1024]{2,1,0:T(8,128)}, f32[27,64,64]{2,1,0:T(8,128)}, bf16[64,1024]{1,0:T(8,128)(2,1)}, bf16[32,2048]{1,0:T(8,128)(2,1)}) custom-call(bf16[8,27,64,128]{3,2,1,0:T(8,128)(2,1)} %get-tuple-element.12.gw, bf16[640,256]{1,0:T(8,128)(2,1)} %get-tuple-element.13.t, bf16[64,1024]{1,0:T(8,128)(2,1)} %get-tuple-element.14.f, ...), custom_call_target="tpu_custom_call" | custom-call | tf_op jit(solution)/shard_map/finish/pallas_call | solution.py:598
where the time goes:
time: 122 us
  Pallas kernels  121 us (99%)
    pallas_call x1, Pallas kernels, mega(): pl.pallas_call(mega_kernel, out_shape=[sds((64, 1024)), sds((32, 2048)),...  113 us
    pallas_call x1, Pallas kernels, finish(): pl.pallas_call(finish_kernel, grid=(9,), out_shape=[sds((27, 64, 1024), F...  8.37 us

commit v1 on v0

--- a/solution.py
+++ b/solution.py
@@ -169,17 +169,31 @@
         put_band(band, ab, jnp.concatenate(w3, axis=0))
 
 
+STOP = None
+
+
+class Done(Exception):
+    pass
+
+
 CHUNKS = [(4 * q, min(4, 27 - 4 * q)) for q in range(7)]
 XF = (0, 1, 2)
 ZF = (3, 4, 5, 6)
 
 
-def mega_kernel(
+def mega_kernel(*refs):
+    try:
+        mega_body(*refs)
+    except Done:
+        pass
+
+
+def mega_body(
     v, cot, w1, w,
-    feat, gvol, tout, gw,
+    feat, gvol, o1, gw,
     vp, vn, cotp, mine, cb, csl, wv, mk, moved, lhs, lhsb, band, bandb, s2o, s2, part, frecv,
     gm, grecv, acc, wacc, pre, ownf, psend, precv, gpn, gp, gn, tbuf, pbuf, pbuf2, own, rbuf, dbuf, rbuf2,
-    wsem, hsem, asem, csem, xsem, msem, ssem, gsem, rsem, psem, nsend, nrecv, ksem, tsem,
+    wsem, hsem, asem, csem, xsem, msem, ssend, srecv, gsem, rsem, psem, nsend, nrecv, ksem, tsem,
 ):
     s, d = where_am_i()
     zh, y, c = d // 8, (d // 2) % 4, d % 2
@@ -187,67 +201,119 @@
     zl = s // 4
     up, down = (d + 1) % 16, (d + 15) % 16
     partner = depth_of(zh, y, 1 - c)
-    wl = pltpu.make_async_copy(w, wv.at[:, c], wsem.at[0])
-    wl.start()
-    barrier(
-        [(s, depth_peer(d, jz, jy, jc)) for jz in range(2) for jy in range(4) for jc in range(2) if (jz, jy, jc) != (0, 0, 0)]
-        + [(sample_peer(s, jz, jx), d) for jz, jx in SAMPS]
-    )
+    yp, ym = depth_of(zh, (y + 1) % 4, c), depth_of(zh, (y + 3) % 4, c)
     late = []
-
-    def spread(src_of, dst, sems, edge):
+    pend = {}
+
+    def stop(k):
+        if STOP == k:
+            for fn in list(pend.values()):
+                fn()
+            for cond, cp in late:
+                wait_late(cond, cp)
+            raise Done
+
+    def wait(k):
+        pend.pop(k)()
+
+    def wait_late(cond, cp):
+        if cond is None:
+            cp.wait_send()
+        else:
+
+            @pl.when(cond)
+            def _():
+                cp.wait_send()
+
+    def go(src, dst, ss, rs, dev):
+        cp = rcopy(src, dst, ss, rs, dev)
+        cp.start()
+        late.append((None, cp))
+
+    def got(ref, ss, rs):
+        rcopy(ref, ref, ss, rs, (s, partner)).wait_recv()
+
+    def spread(src_of, dst, sems):
         k = d % 8
         for i, (jz, jy) in enumerate([(0, 0)] + CHIPS):
             t = depth_of((zh + jz) % 2, (y + jy) % 4, zh)
-            cp = rcopy(src_of(t // 2), dst(k + edge), sems.at[i], sems.at[16 + k], (s, t))
             if i:
-                cp.start()
-                late.append((None, cp))
+                go(src_of(t // 2), dst(k + 1), sems.at[i], sems.at[16 + k], (s, t))
             else:
+                cp = rcopy(src_of(t // 2), dst(k + 1), sems.at[i], sems.at[16 + k], (s, t))
 
                 @pl.when(t != d)
                 def _(cp=cp):
                     cp.start()
 
                 late.append((t != d, cp))
-        if edge:
-            rim = (d == 7) | (d == 8)
-            for i, (jz, jy) in enumerate(CHIPS):
-                t = depth_of((zh + jz) % 2, (y + jy) % 4, 1 - zh)
-                cp = rcopy(src_of(t // 2), dst(zh * 9), sems.at[8 + i], sems.at[24], (s, t))
-
-                @pl.when(rim)
-                def _(cp=cp):
-                    cp.start()
-
-                late.append((rim, cp))
-
-    def spread_local(value, dst_ref, edge):
+        rim = (d == 7) | (d == 8)
+        for i, (jz, jy) in enumerate(CHIPS):
+            t = depth_of((zh + jz) % 2, (y + jy) % 4, 1 - zh)
+            cp = rcopy(src_of(t // 2), dst(zh * 9), sems.at[8 + i], sems.at[24], (s, t))
+
+            @pl.when(rim)
+            def _(cp=cp):
+                cp.start()
+
+            late.append((rim, cp))
+
+    def spread_wait(dst, sems):
+        for k in range(8):
+
+            @pl.when(8 * c + k != d)
+            def _(k=k):
+                got(dst(k + 1), sems.at[0], sems.at[16 + k])
+
+        q = 9 - 9 * c
+
+        @pl.when(8 - c != d)
+        def _():
+            got(dst(q), sems.at[0], sems.at[24])
+
+    def home_send(src, buf, sems, edge):
+        k = d % 8 + edge
+        here, there = depth_of(zh, y, zh), depth_of(1 - zh, y, zh)
+        go(src, buf.at[k], sems.at[1], sems.at[4 + c], (s, there))
+        cp = rcopy(src, buf.at[k], sems.at[0], sems.at[4 + c], (s, here))
+
+        @pl.when(c != zh)
+        def _():
+            cp.start()
+
+        late.append((c != zh, cp))
+
         @pl.when(c == zh)
         def _():
-            dst_ref(d % 8 + edge, value)
-
-        if edge:
-
-            @pl.when((d == 7) | (d == 8))
-            def _():
-                dst_ref(zh * 9, value)
-
-    def spread_wait(dst, sems, edge):
-        for k in range(8):
-
-            @pl.when(8 * c + k != d)
-            def _(k=k):
-                rcopy(dst(k + edge), dst(k + edge), sems.at[0], sems.at[16 + k], (s, partner)).wait_recv()
-
-        if edge:
-            q = 9 - 9 * c
-
-            @pl.when(8 - c != d)
-            def _():
-                rcopy(dst(q), dst(q), sems.at[0], sems.at[24], (s, partner)).wait_recv()
-
-    def to_owner(src, dst, sems, lo=0):
+            buf[k] = src[...]
+
+    def home_wait(buf, sems, edge):
+        for j in range(2):
+
+            @pl.when((zh != c) | (c != j))
+            def _(j=j):
+                got(buf.at[2 * y + j + edge], sems.at[0], sems.at[4 + j])
+
+    def ring_send(buf, sems, edge):
+        two = buf.at[pl.ds(2 * y + edge, 2)]
+        go(two, two, sems.at[2], sems.at[6], (s, yp))
+        go(two, two, sems.at[3], sems.at[7], (s, ym))
+
+    def ring_relay(buf, sems, edge):
+        lo, hi = (y + 3) % 4, (y + 1) % 4
+        got(buf.at[pl.ds(2 * lo + edge, 2)], sems.at[2], sems.at[6])
+        one = buf.at[2 * lo + edge]
+        go(one, one, sems.at[8], sems.at[10], (s, yp))
+        got(buf.at[pl.ds(2 * hi + edge, 2)], sems.at[3], sems.at[7])
+        one = buf.at[2 * hi + 1 + edge]
+        go(one, one, sems.at[9], sems.at[11], (s, ym))
+
+    def ring_wait(buf, sems, edge):
+        far = (y + 2) % 4
+        got(buf.at[2 * far + edge], sems.at[8], sems.at[10])
+        got(buf.at[2 * far + 1 + edge], sems.at[9], sems.at[11])
+
+    def to_owner(src, dst, sems):
         for i in range(8):
             p = 8 * c + i
             cp = rcopy(src.at[i], dst.at[m], sems.at[i], sems.at[8 + m], (s, p))
@@ -267,34 +333,129 @@
 
             @pl.when(2 * j + zh != d)
             def _(j=j):
-                rcopy(dst.at[j], dst.at[j], sems.at[0], sems.at[8 + j], (s, partner)).wait_recv()
+                got(dst.at[j], sems.at[0], sems.at[8 + j])
+
+    xp, xm, x2 = sample_peer(s, 0, 1), sample_peer(s, 0, 3), sample_peer(s, 0, 2)
+    zo, oxp, oxm, ox2 = sample_peer(s, 1, 0), sample_peer(s, 1, 1), sample_peer(s, 1, 3), sample_peer(s, 1, 2)
+
+    class Gather:
+        def __init__(self, ref, xf, zf, ss, rs):
+            self.ref, self.xf, self.zf, self.ss, self.rs = ref, xf, zf, ss, rs
+
+        def send(self, q, kind, block, dev):
+            r = self.ref(block, q)
+            go(r, r, self.ss.at[7 * q + kind], self.rs.at[7 * q + kind], (dev, d))
+
+        def recv(self, q, kind, block):
+            got(self.ref(block, q), self.ss.at[7 * q + kind], self.rs.at[7 * q + kind])
+
+        def start(self, q):
+            if q in self.zf:
+                self.send(q, 0, s, zo)
+            self.send(q, 1, s, xp)
+            self.send(q, 2, s, xm)
+
+        def start_z(self):
+            for q in self.xf:
+                self.send(q, 0, s, zo)
+
+        def near(self, q):
+            self.recv(q, 1, xm)
+            if q % 2 == 0:
+                self.send(q, 3, xm, xp)
+            if q in self.xf:
+                self.send(q, 4, xm, zo)
+            self.recv(q, 2, xp)
+            if q % 2:
+                self.send(q, 3, xp, xm)
+            if q in self.xf:
+                self.send(q, 5, xp, zo)
+
+        def across(self, q):
+            self.recv(q, 0, zo)
+            self.send(q, 4, zo, xp)
+            self.send(q, 5, zo, xm)
+
+        def far(self, q):
+            self.recv(q, 3, x2)
+            self.send(q, 6, x2, zo)
+
+        def turn(self, q):
+            self.recv(q, 4, oxm)
+            if q % 2 == 0:
+                self.send(q, 6, oxm, xp)
+            self.recv(q, 5, oxp)
+            if q % 2:
+                self.send(q, 6, oxp, xm)
+
+        def finish(self):
+            for q in self.xf:
+                self.recv(q, 0, zo)
+                self.recv(q, 4, oxm)
+                self.recv(q, 5, oxp)
+                self.recv(q, 6, ox2)
+            for q in self.zf:
+                self.recv(q, 3, x2)
+                self.recv(q, 6, ox2)
+
+        def rest(self):
+            for q in self.xf:
+                self.near(q)
+            for q in self.zf:
+                self.across(q)
+            for q in self.zf:
+                self.near(q)
+            for q in self.xf:
+                self.far(q)
+            for q in self.zf:
+                self.turn(q)
+            self.finish()
+
+    agm = Gather(lambda b, q: mk.at[b, pl.ds(1 - c + 3 * q, 3)], (0,), (1, 2), ssend, srecv)
+    agw = Gather(
+        lambda b, q: gw.at[pl.ds(*CHUNKS[q]), :, pl.ds(pl.multiple_of(b * 128, 128), 128)], XF, ZF, nsend, nrecv
+    )
+
+    wl = pltpu.make_async_copy(w, wv.at[:, c], wsem.at[0])
+    wl.start()
+    pend["wl"] = wl.wait
+    bar = pltpu.get_barrier_semaphore()
+    friends = [
+        (s, depth_peer(d, jz, jy, jc)) for jz in range(2) for jy in range(4) for jc in range(2) if (jz, jy, jc) != (0, 0, 0)
+    ] + [(sample_peer(s, jz, jx), d) for jz, jx in SAMPS]
+    for dev in friends:
+        pl.semaphore_signal(bar, inc=1, device_id=dev, device_id_type=MESH)
+    perm64 = onehot((64, 64), lambda u, q: q == (u % 8) * 8 + u // 8)
+    cotp[...] = dot(perm64, cot[...]).astype(BF16)
+    mine[s] = cotp[:, pl.ds(pl.multiple_of(s * 128, 128), 128)]
+    cb[9 * c] = jnp.zeros((64, 1024), BF16)
+    mk[:, 9 * c] = jnp.zeros((8, 64, 128), BF16)
+    fill_band(band, w1)
+    pl.semaphore_wait(bar, len(friends))
+    stop(0)
 
     halo = [rcopy(v, vp, hsem.at[0], hsem.at[1], (s, up)), rcopy(v, vn, hsem.at[2], hsem.at[3], (s, down))]
     for h in halo:
         h.start()
+    pend["halo"] = lambda: [h.wait() for h in halo]
+    home_send(cotp, cb, csem, 1)
+    for i, (jz, jx) in enumerate(SAMPS):
+        t = sample_peer(s, jz, jx)
+        go(cotp.at[:, pl.ds(pl.multiple_of(t * 128, 128), 128)], mine.at[s], asem.at[i], asem.at[7 + i], (t, d))
     wx = rcopy(w, wv.at[:, c], wsem.at[1], wsem.at[2], (s, partner))
     wx.start()
-    perm64 = onehot((64, 64), lambda u, q: q == (u % 8) * 8 + u // 8)
-    cotp[...] = dot(perm64, cot[...]).astype(BF16)
-    for i, (jz, jx) in enumerate(SAMPS):
-        t = sample_peer(s, jz, jx)
-        cp = rcopy(cotp.at[:, pl.ds(pl.multiple_of(t * 128, 128), 128)], mine.at[s], asem.at[i], asem.at[7 + i], (t, d))
-        cp.start()
-        late.append((None, cp))
-    spread(lambda t: cotp, lambda k: cb.at[k], csem, 1)
-
-    def put_cb(k, value):
-        cb[k] = value
-
-    spread_local(cotp[...], put_cb, 1)
-    mine[s] = cotp[:, pl.ds(pl.multiple_of(s * 128, 128), 128)]
-    cb[9 * c] = jnp.zeros((64, 1024), BF16)
-    mk[:, 9 * c] = jnp.zeros((8, 64, 128), BF16)
-
-    fill_band(band, w1)
+    pend["wx"] = wx.wait
+
+    def mine_wait():
+        for i, (jz, jx) in enumerate(SAMPS):
+            got(mine.at[sample_src(s, jz, jx)], asem.at[i], asem.at[7 + i])
+
+    pend["mine"] = mine_wait
+
     perms = [onehot((32, 32), lambda rho, i, b=b: i == nat(rho) + b - 1) for b in range(3)]
-    for h in halo:
-        h.wait()
+    wait("halo")
+    home_wait(cb, csem, 1)
+    ring_send(cb, csem, 1)
     fill_rows(lhs, edge_planes(vp[...], v[...], vn[...], d), perms)
     res = dot(lhs[...], band[...])
     for r in range(4):
@@ -303,36 +464,66 @@
         hid = (0.5 * z * (1.0 + gelu_parts(z))).astype(BF16)
         moved[2 * r] = hid[:, 0:128]
         moved[2 * r + 1] = hid[:, 128:256]
-    spread(lambda t: moved.at[t], lambda k: mk.at[s, k], msem, 1)
-
-    def put_mk(k, value):
-        mk[s, k] = value
-
-    spread_local(moved[m], put_mk, 1)
-
-    for i, (jz, jx) in enumerate(SAMPS):
-        t = sample_src(s, jz, jx)
-        rcopy(mine.at[t], mine.at[t], asem.at[i], asem.at[7 + i], (t, d)).wait_recv()
-    spread(lambda t: mine, lambda k: csl.at[k], xsem, 0)
-
-    def put_csl(k, value):
-        csl[k] = value
-
-    spread_local(mine[...], put_csl, 0)
+    spread(lambda t: moved.at[t], lambda k: mk.at[s, k], msem)
+    pend["mk"] = lambda: spread_wait(lambda k: mk.at[s, k], msem)
+
+    @pl.when(c == zh)
+    def _():
+        mk[s, d % 8 + 1] = moved[m]
+
+    @pl.when((d == 7) | (d == 8))
+    def _():
+        mk[s, zh * 9] = moved[m]
+
+    wait("mine")
+    home_send(mine, csl, xsem, 0)
+    if STOP == 1:
+        pend["a"] = lambda: (ring_relay(cb, csem, 1), home_wait(csl, xsem, 0), ring_wait(cb, csem, 1))
+    stop(1)
     fill_band_back(bandb, w1)
+    ring_relay(cb, csem, 1)
+
+    wait("mk")
+    for q in range(3):
+        agm.start(q)
+    agm.start_z()
+    home_wait(csl, xsem, 0)
+    ring_send(csl, xsem, 0)
+    if STOP == 2:
+        pend["a"] = lambda: (ring_relay(csl, xsem, 0), ring_wait(cb, csem, 1), ring_wait(csl, xsem, 0), agm.rest())
+    stop(2)
+    taps10(mk[s], s2o)
     wacc[...] = jnp.zeros_like(wacc)
-
-    spread_wait(lambda k: mk.at[s, k], msem, 1)
-    nine = pl.ds(1 - c, 9)
-    for i in range(1, 8):
-        cp = rcopy(mk.at[s, nine], mk.at[s, nine], ssem.at[i - 1], ssem.at[6 + i], (sample_peer(s, i // 4, i % 4), d))
-        cp.start()
-        late.append((None, cp))
-    taps10(mk[s], s2o)
-
-    wl.wait()
-    wx.wait()
-    spread_wait(lambda k: cb.at[k], csem, 1)
+    ring_wait(cb, csem, 1)
+    rim_out = cb.at[8 - 7 * c]
+    go(rim_out, cb.at[9 * c], csem.at[12], csem.at[13], (s, partner))
+    agm.near(0)
+    agm.across(1)
+    agm.across(2)
+    wait("wl")
+    wait("wx")
+
+    def fwd(i, _):
+        tot = jnp.zeros((256, 1024), F32)
+        for a in range(3):
+            tot = tot + dot(s2o[pl.ds(4 * i + a, 4)].reshape(256, 1152), wv[9 * a : 9 * a + 9].reshape(1152, 1024))
+        part[pl.ds(4 * i, 4)] = tot.astype(BF16).reshape(4, 64, 1024)
+        return 0
+
+    fwd(0, 0)
+    agm.near(1)
+    agm.near(2)
+    agm.far(0)
+    ring_relay(csl, xsem, 0)
+    fwd(1, 0)
+    agm.turn(1)
+    agm.turn(2)
+    to_owner(part, frecv, rsem)
+    pend["part"] = lambda: owner_wait(frecv, rsem)
+    got(cb.at[9 - 9 * c], csem.at[12], csem.at[13])
+    if STOP == 3:
+        pend["a"] = lambda: (ring_wait(csl, xsem, 0), agm.finish())
+    stop(3)
 
     def back(i, _):
         tot = jnp.zeros((512, 384), F32)
@@ -353,8 +544,11 @@
         total = total + row_shift(inner.reshape(512, 128), 2 - b).reshape(8, 64, 128)
     gm[...] = total.astype(BF16)
     to_owner(gm, grecv, gsem)
-
-    spread_wait(lambda k: csl.at[k], xsem, 0)
+    pend["gm"] = lambda: owner_wait(grecv, gsem)
+
+    ring_wait(csl, xsem, 0)
+    agm.finish()
+    stop(4)
 
     def wpart(t, ref):
         ct = jnp.transpose(csl[:, t].reshape(512, 128).astype(F32)).astype(BF16)
@@ -365,12 +559,12 @@
 
     def wgrad(i, _):
         t = ((zl + i // 4) % 2) * 4 + (s % 4 + 4 - i % 4) % 4
-        rcopy(mk.at[t, nine], mk.at[t, nine], ssem.at[i - 1], ssem.at[6 + i], (s, partner)).wait_recv()
         taps10(mk[t], s2)
         wpart(t, s2)
         return 0
 
     lax.fori_loop(1, 8, wgrad, 0)
+    stop(5)
 
     pcp = []
     for q, (lo, n) in enumerate(CHUNKS):
@@ -381,35 +575,18 @@
         cp = rcopy(psend.at[pl.ds(lo, n)], precv.at[pl.ds(lo, n)], psem.at[q], psem.at[7 + q], (s, partner))
         cp.start()
         pcp.append(cp)
-
-    xp, xm, zo = sample_peer(s, 0, 1), sample_peer(s, 0, 3), sample_peer(s, 1, 0)
-    x2 = sample_peer(s, 0, 2)
-    oxp, oxm, ox2 = sample_peer(s, 1, 1), sample_peer(s, 1, 3), sample_peer(s, 1, 2)
-
-    def nsem(q, kind):
-        return nsend.at[7 * q + kind], nrecv.at[7 * q + kind]
-
-    def send(q, kind, block, dev):
-        ref = gw.at[block, pl.ds(*CHUNKS[q])]
-        cp = rcopy(ref, ref, *nsem(q, kind), (dev, d))
-        cp.start()
-        late.append((None, cp))
-
-    def recv(q, kind, block):
-        ref = gw.at[block, pl.ds(*CHUNKS[q])]
-        rcopy(ref, ref, *nsem(q, kind), (s, partner)).wait_recv()
-
     for q, (lo, n) in enumerate(CHUNKS):
         pcp[q].wait()
-        gw[s, pl.ds(lo, n)] = (ownf[pl.ds(lo, n)] + precv[pl.ds(lo, n)].astype(F32)).astype(BF16)
-        if q in ZF:
-            send(q, 0, s, zo)
-        send(q, 1, s, xp)
-        send(q, 2, s, xm)
-    for q in XF:
-        send(q, 0, s, zo)
-
-    owner_wait(grecv, gsem)
+        gw[pl.ds(lo, n), :, pl.ds(pl.multiple_of(s * 128, 128), 128)] = (
+            ownf[pl.ds(lo, n)] + precv[pl.ds(lo, n)].astype(F32)
+        ).astype(BF16)
+        agw.start(q)
+    agw.start_z()
+    if STOP == 6:
+        agw.rest()
+    stop(6)
+
+    wait("gm")
     gpf = []
     for r in range(4):
         z = pre[r]
@@ -422,6 +599,7 @@
     ghalo = [rcopy(gpn, gp, hsem.at[4], hsem.at[5], (s, up)), rcopy(gpn, gn, hsem.at[6], hsem.at[7], (s, down))]
     for h in ghalo:
         h.start()
+    pend["ghalo"] = lambda: [h.wait() for h in ghalo]
 
     gx = jnp.concatenate([gpn[:, 256 * j : 256 * j + 256] for j in range(8)], axis=0)
     gt = jnp.transpose(gx.astype(F32)).astype(BF16)
@@ -435,17 +613,8 @@
     lane2 = pl.ds(pl.multiple_of(128 - c * 128, 128), 128)
     k1 = rcopy(tbuf.at[:, lane2], pbuf, ksem.at[0], ksem.at[1], (s, partner))
     k1.start()
-
     for q in XF:
-        recv(q, 1, xm)
-        if q % 2 == 0:
-            send(q, 3, xm, xp)
-        send(q, 4, xm, zo)
-        recv(q, 2, xp)
-        if q % 2:
-            send(q, 3, xp, xm)
-        send(q, 5, xp, zo)
-
+        agw.near(q)
     k1.wait()
     own[...] = (tbuf[:, lane].astype(F32) + pbuf[...].astype(F32)).astype(BF16)
     k2s = []
@@ -453,33 +622,8 @@
         t = depth_peer(d, jz, jy, 0)
         k2s.append(rcopy(own.at[pl.ds(pl.multiple_of((t // 2) * 80, 16), 80)], rbuf.at[i], tsem.at[i], tsem.at[7 + i], (s, t)))
         k2s[-1].start()
-
     for q in ZF:
-        recv(q, 0, zo)
-        send(q, 4, zo, xp)
-        send(q, 5, zo, xm)
-
-    def fwd(i, _):
-        tot = jnp.zeros((256, 1024), F32)
-        for a in range(3):
-            tot = tot + dot(s2o[pl.ds(4 * i + a, 4)].reshape(256, 1152), wv[9 * a : 9 * a + 9].reshape(1152, 1024))
-        part[pl.ds(4 * i, 4)] = tot.astype(BF16).reshape(4, 64, 1024)
-        return 0
-
-    lax.fori_loop(0, 2, fwd, 0)
-    to_owner(part, frecv, rsem)
-
-    for q in ZF:
-        recv(q, 1, xm)
-        if q % 2 == 0:
-            send(q, 3, xm, xp)
-        recv(q, 2, xp)
-        if q % 2:
-            send(q, 3, xp, xm)
-    for q in XF:
-        recv(q, 3, x2)
-        send(q, 6, x2, zo)
-
+        agw.across(q)
     piece = pl.ds(pl.multiple_of(m * 80, 16), 80)
     tot = own[piece].astype(F32)
     for i in range(7):
@@ -490,23 +634,37 @@
     for i, (jz, jx) in enumerate(SAMPS):
         k3s.append(rcopy(dbuf.at[7], dbuf.at[i], tsem.at[14 + i], tsem.at[21 + i], (sample_peer(s, jz, jx), d)))
         k3s[-1].start()
-
-    for h in ghalo:
-        h.wait()
+    if STOP == 7:
+        for q in ZF:
+            agw.near(q)
+        for q in XF:
+            agw.far(q)
+        for q in ZF:
+            agw.turn(q)
+        agw.finish()
+        for x in k3s:
+            x.wait()
+    stop(7)
+
+    wait("ghalo")
     perms = [onehot((32, 32), lambda u, q, b=b: nat(q) == nat(u) + b - 1) for b in range(3)]
     perms[1] = None
     fill_rows(lhsb, edge_planes(gp[...], gpn[...], gn[...], d), perms)
     res = dot(lhsb[...], bandb[...]).astype(BF16)
     wide = jnp.concatenate([res[32 * j : 32 * j + 32] for j in range(8)], axis=1)
     gvol[...] = dot(onehot((32, 32), lambda i, q: nat(q) == i), wide).astype(BF16)
-
     for q in ZF:
-        recv(q, 4, oxm)
-        if q % 2 == 0:
-            send(q, 6, oxm, xp)
-        recv(q, 5, oxp)
-        if q % 2:
-            send(q, 6, oxp, xm)
+        agw.near(q)
+    for q in XF:
+        agw.far(q)
+
+    wait("part")
+    tot = frecv[0].astype(F32)
+    for i in range(1, 8):
+        tot = tot + frecv[i].astype(F32)
+    feat[...] = dot(perm64, tot.astype(BF16)).astype(BF16)
+    for q in ZF:
+        agw.turn(q)
 
     for x in k3s:
         x.wait()
@@ -521,38 +679,20 @@
     for i, (jz, jy) in enumerate(CHIPS):
         k4s.append(rcopy(own.at[piece], rbuf2.at[i], tsem.at[28 + i], tsem.at[35 + i], (s, depth_peer(d, jz, jy, 0))))
         k4s[-1].start()
-
-    owner_wait(frecv, rsem)
-    tot = frecv[0].astype(F32)
-    for i in range(1, 8):
-        tot = tot + frecv[i].astype(F32)
-    feat[...] = dot(perm64, tot.astype(BF16)).astype(BF16)
-
     for i, (jz, jy) in enumerate(CHIPS):
         k4s[i].wait()
         own[pl.ds(pl.multiple_of((depth_src(d, jz, jy, 0) // 2) * 80, 16), 80)] = rbuf2[i]
     k5 = rcopy(own, pbuf2, ksem.at[2], ksem.at[3], (s, partner))
     k5.start()
-    tout[:, lane] = own[...]
     k5.wait()
-    tout[:, lane2] = pbuf2[...]
-
-    for q in XF:
-        recv(q, 0, zo)
-        recv(q, 4, oxm)
-        recv(q, 5, oxp)
-        recv(q, 6, ox2)
-    for q in ZF:
-        recv(q, 3, x2)
-        recv(q, 6, ox2)
+    left = jnp.where(c == 0, own[...], pbuf2[...]).astype(F32)
+    right = jnp.where(c == 0, pbuf2[...], own[...]).astype(F32)
+    for ab in range(9):
+        both = jnp.concatenate([left[64 * ab : 64 * ab + 64], right[64 * ab : 64 * ab + 64]], axis=1)
+        o1[3 * ab : 3 * ab + 3] = jnp.transpose(both)[0:192].reshape(3, 64, 64)
+    agw.finish()
     for cond, cp in late:
-        if cond is None:
-            cp.wait_send()
-        else:
-
-            @pl.when(cond)
-            def _(cp=cp):
-                cp.wait_send()
+        wait_late(cond, cp)
 
 
 def mega(v, cot, w1, w):
@@ -566,12 +706,12 @@
         vm(8, 64, 128), vm(8, 64, 128), vf(9, 512, 128), vf(128, 3456), vf(4, 64, 256), vf(27, 64, 128),
         vm(27, 64, 128), vm(27, 64, 128), vm(32, 2048), vm(32, 2048), vm(32, 2048), vm(640, 256), vm(640, 128),
         vm(640, 128), vm(640, 128), vm(7, 80, 128), vm(8, 80, 128), vm(7, 80, 128),
-        dma((3,)), dma((8,)), dma((14,)), dma((25,)), dma((25,)), dma((25,)), dma((14,)), dma((16,)), dma((16,)),
+        dma((3,)), dma((8,)), dma((14,)), dma((14,)), dma((14,)), dma((25,)), dma((21,)), dma((21,)), dma((16,)), dma((16,)),
         dma((14,)), dma((49,)), dma((49,)), dma((4,)), dma((42,)),
     ]
     return pl.pallas_call(
         mega_kernel,
-        out_shape=[sds((64, 1024)), sds((32, 2048)), sds((640, 256)), sds((8, 27, 64, 128))],
+        out_shape=[sds((64, 1024)), sds((32, 2048)), sds((27, 64, 64), F32), sds((27, 64, 1024))],
         in_specs=[VM, VM, VM, ANY],
         out_specs=[VM] * 4,
         scratch_shapes=scratch,
@@ -581,16 +721,13 @@
 
 
 def finish_kernel(gw, t, f, g, o2, o1, of, og):
-    for q in range(8):
-        o2[:, :, 128 * q : 128 * q + 128] = gw[q].astype(F32)
+    o2[...] = gw[...].astype(F32)
 
     @pl.when(pl.program_id(0) == 0)
     def _():
         of[...] = f[...]
         og[...] = g[...]
-        for ab in range(9):
-            x = jnp.transpose(t[64 * ab : 64 * ab + 64].astype(F32))
-            o1[3 * ab : 3 * ab + 3] = x[0:192].reshape(3, 64, 64)
+        o1[...] = t[...]
 
 
 def finish(gw, t, f, g):
@@ -599,7 +736,7 @@
         finish_kernel,
         grid=(9,),
         out_shape=[sds((27, 64, 1024), F32), sds((27, 64, 64), F32), sds((64, 1024)), sds((32, 2048))],
-        in_specs=[pl.BlockSpec((8, 3, 64, 128), lambda i: (0, i, 0, 0)), whole(640, 256), whole(64, 1024), whole(32, 2048)],
+        in_specs=[pl.BlockSpec((3, 64, 1024), lambda i: (i, 0, 0)), whole(27, 64, 64), whole(64, 1024), whole(32, 2048)],
         out_specs=[pl.BlockSpec((3, 64, 1024), lambda i: (i, 0, 0)), whole(27, 64, 64), whole(64, 1024), whole(32, 2048)],
         compiler_params=pltpu.CompilerParams(vmem_limit_bytes=LIMIT),
         name="finish",
@@ -607,8 +744,8 @@
 
 
 def on_device(volume, conv1_weight, conv2_weight, cotangent):
-    feat, gvol, tall, gw = mega(volume.reshape(32, 2048), cotangent.reshape(64, 1024), conv1_weight, conv2_weight)
-    o2, o1, feat, gvol = finish(gw, tall, feat, gvol)
+    feat, gvol, o1, gw = mega(volume.reshape(32, 2048), cotangent.reshape(64, 1024), conv1_weight, conv2_weight)
+    o2, o1, feat, gvol = finish(gw, o1, feat, gvol)
     return feat.reshape(1, 1, 8, 8, 1024), gvol.reshape(1, 1, 32, 2048), o1, o2
 
 

time: 122 us -> 104 us (0.85)
  Pallas kernels: 121 us -> 103 us
    pallas_call x1, Pallas kernels: 113 us -> 94.9 us  [mega(): pl.pallas_call(mega_kernel, out_shape=[sds((64, 1024)), sds((32, 2048)),...]
where the time goes in v1:
time: 104 us
  Pallas kernels  103 us (99%)
    pallas_call x1, Pallas kernels, mega(): pl.pallas_call(mega_kernel, out_shape=[sds((64, 1024)), sds((32, 2048)),...  94.9 us
    pallas_call x1, Pallas kernels, finish(): pl.pallas_call(finish_kernel, grid=(9,), out_shape=[sds((27, 64, 1024), F...  8.22 us

profile of v1, /device:TPU:1, one launch (start us, length us, event | category | flops | bytes accessed | tf_op | source)
XLA Modules:
  0.0 103.8 jit_solution(13157974811350936707)
XLA Ops:
  0.6 94.9 %step.1 = (bf16[64,1024]{1,0:T(8,128)(2,1)}, bf16[32,2048]{1,0:T(8,128)(2,1)}, f32[27,64,64]{2,1,0:T(8,128)}, bf16[27,64,1024]{2,1,0:T(8,128)(2,1)}) custom-call(bf16[32,2048]{1,0:T(8,128)(2,1)} %bitcast.4, bf16[64,1024]{1,0:T(8,128)(2,1)} %bitcast.5, bf16[27,64,64]{2,1,0:T(8,128)(2,1)} %refs_2_.1, bf16[27,64,1024]{2,1,0:T(8,128)(2,1)} %refs_3_.1), custom_call_target="tpu_custom_call" | custom-call | tf_op jit(solution)/shard_map/step/pallas_call | solution.py:712
  95.6 8.2 %finish.1 = (f32[27,64,1024]{2,1,0:T(8,128)}, f32[27,64,64]{2,1,0:T(8,128)}, bf16[64,1024]{1,0:T(8,128)(2,1)}, bf16[32,2048]{1,0:T(8,128)(2,1)}) custom-call(bf16[27,64,1024]{2,1,0:T(8,128)(2,1)} %get-tuple-element.12.gw, f32[27,64,64]{2,1,0:T(8,128)} %get-tuple-element.13.t, bf16[64,1024]{1,0:T(8,128)(2,1)} %get-tuple-element.14.f, ...), custom_call_target="tpu_custom_call" | custom-call | tf_op jit(solution)/shard_map/finish/pallas_call | solution.py:735

commit v2 on v1

--- a/solution.py
+++ b/solution.py
@@ -191,9 +191,9 @@
 def mega_body(
     v, cot, w1, w,
     feat, gvol, o1, gw,
-    vp, vn, cotp, mine, cb, csl, wv, mk, moved, lhs, lhsb, band, bandb, s2o, s2, part, frecv,
-    gm, grecv, acc, wacc, pre, ownf, psend, precv, gpn, gp, gn, tbuf, pbuf, pbuf2, own, rbuf, dbuf, rbuf2,
-    wsem, hsem, asem, csem, xsem, msem, ssend, srecv, gsem, rsem, psem, nsend, nrecv, ksem, tsem,
+    vp, vn, cotp, mine, cb, csl, wv, mk, moved, lhs, lhsb, band, bandb, s2o, s2, part, zrecv, frecv,
+    gm, grecv, acc, wacc, pre, ownf, psend, precv, gpn, gp, gn, tbuf, tall, rbuf, dbuf,
+    wsem, hsem, asem, csem, xsem, msem, ssend, srecv, gsem, rsem, psem, nsend, nrecv, tsem,
 ):
     s, d = where_am_i()
     zh, y, c = d // 8, (d // 2) % 4, d % 2
@@ -313,8 +313,53 @@
         got(buf.at[2 * far + edge], sems.at[8], sems.at[10])
         got(buf.at[2 * far + 1 + edge], sems.at[9], sems.at[11])
 
-    def to_owner(src, dst, sems):
+    def features_z():
+        cp = rcopy(part, zrecv, rsem.at[0], rsem.at[1], (s, depth_of(1 - zh, y, c)))
+
+        @pl.when(zh != c)
+        def _():
+            cp.start()
+
+        late.append((zh != c, cp))
+
+    def features_y():
+        cps = []
         for i in range(8):
+            if i < 2:
+                q, dev = 2 * y + i, depth_of(zh, y, i)
+            else:
+                q = 2 * ((y + i // 2) % 4) + i % 2
+                dev = depth_of(zh, (y + i // 2) % 4, i % 2)
+            cps.append((dev != d, rcopy(part.at[q], frecv.at[y], rsem.at[2 + i], rsem.at[10 + y], (s, dev))))
+
+        @pl.when(zh == c)
+        def _():
+            got(zrecv, rsem.at[0], rsem.at[1])
+            for i in range(8):
+                part[i] = (part[i].astype(F32) + zrecv[i].astype(F32)).astype(BF16)
+            for i, (cond, cp) in enumerate(cps):
+                if i >= 2:
+                    cp.start()
+                else:
+
+                    @pl.when(cond)
+                    def _(cp=cp):
+                        cp.start()
+
+            frecv[y] = part[2 * y + c]
+
+        for cond, cp in cps:
+            late.append(((zh == c) & cond, cp))
+
+    def features_wait():
+        for j in range(4):
+
+            @pl.when((j != y) | (zh != c))
+            def _(j=j):
+                got(frecv.at[j], rsem.at[0], rsem.at[10 + j])
+
+    def to_owner(src, dst, sems, which=range(8)):
+        for i in which:
             p = 8 * c + i
             cp = rcopy(src.at[i], dst.at[m], sems.at[i], sems.at[8 + m], (s, p))
 
@@ -454,8 +499,6 @@
 
     perms = [onehot((32, 32), lambda rho, i, b=b: i == nat(rho) + b - 1) for b in range(3)]
     wait("halo")
-    home_wait(cb, csem, 1)
-    ring_send(cb, csem, 1)
     fill_rows(lhs, edge_planes(vp[...], v[...], vn[...], d), perms)
     res = dot(lhs[...], band[...])
     for r in range(4):
@@ -477,52 +520,74 @@
 
     wait("mine")
     home_send(mine, csl, xsem, 0)
-    if STOP == 1:
-        pend["a"] = lambda: (ring_relay(cb, csem, 1), home_wait(csl, xsem, 0), ring_wait(cb, csem, 1))
-    stop(1)
     fill_band_back(bandb, w1)
-    ring_relay(cb, csem, 1)
+    wacc[...] = jnp.zeros_like(wacc)
+    home_wait(csl, xsem, 0)
+    ring_send(csl, xsem, 0)
 
     wait("mk")
     for q in range(3):
         agm.start(q)
     agm.start_z()
-    home_wait(csl, xsem, 0)
-    ring_send(csl, xsem, 0)
-    if STOP == 2:
-        pend["a"] = lambda: (ring_relay(csl, xsem, 0), ring_wait(cb, csem, 1), ring_wait(csl, xsem, 0), agm.rest())
-    stop(2)
+    if STOP == 1:
+        pend["a"] = lambda: (ring_relay(csl, xsem, 0), home_wait(cb, csem, 1), ring_wait(csl, xsem, 0), agm.rest())
+    stop(1)
     taps10(mk[s], s2o)
-    wacc[...] = jnp.zeros_like(wacc)
-    ring_wait(cb, csem, 1)
-    rim_out = cb.at[8 - 7 * c]
-    go(rim_out, cb.at[9 * c], csem.at[12], csem.at[13], (s, partner))
+    wait("wl")
+    wait("wx")
+
+    def fwd(i):
+        tot = jnp.zeros((256, 1024), F32)
+        for a in range(3):
+            tot = tot + dot(s2o[4 * i + a : 4 * i + a + 4].reshape(256, 1152), wv[9 * a : 9 * a + 9].reshape(1152, 1024))
+        part[4 * i : 4 * i + 4] = tot.astype(BF16).reshape(4, 64, 1024)
+
+    fwd(0)
+    ring_relay(csl, xsem, 0)
+    home_wait(cb, csem, 1)
+    ring_send(cb, csem, 1)
     agm.near(0)
     agm.across(1)
     agm.across(2)
-    wait("wl")
-    wait("wx")
-
-    def fwd(i, _):
-        tot = jnp.zeros((256, 1024), F32)
-        for a in range(3):
-            tot = tot + dot(s2o[pl.ds(4 * i + a, 4)].reshape(256, 1152), wv[9 * a : 9 * a + 9].reshape(1152, 1024))
-        part[pl.ds(4 * i, 4)] = tot.astype(BF16).reshape(4, 64, 1024)
-        return 0
-
-    fwd(0, 0)
+    fwd(1)
     agm.near(1)
     agm.near(2)
     agm.far(0)
-    ring_relay(csl, xsem, 0)
-    fwd(1, 0)
+    features_z()
+
+    def fz():
+        @pl.when(zh == c)
+        def _():
+            got(zrecv, rsem.at[0], rsem.at[1])
+
+    pend["fz"] = fz
+    ring_wait(csl, xsem, 0)
+
+    def wpart(t, ref):
+        ct = jnp.transpose(csl[:, t].reshape(512, 128).astype(F32)).astype(BF16)
+        for a in range(3):
+            wacc[:, 1152 * a : 1152 * a + 1152] += dot(ct, ref[a : a + 8].reshape(512, 1152))
+
+    def wgrad(i, _):
+        j = jnp.where(i == 2, 3, jnp.where(i == 3, 2, i))
+        t = ((zl + j // 4) % 2) * 4 + (s % 4 + 4 - j % 4) % 4
+        taps10(mk[t], s2)
+        wpart(t, s2)
+        return 0
+
+    wpart(s, s2o)
     agm.turn(1)
     agm.turn(2)
-    to_owner(part, frecv, rsem)
-    pend["part"] = lambda: owner_wait(frecv, rsem)
+    ring_relay(cb, csem, 1)
+    lax.fori_loop(1, 3, wgrad, 0)
+    if STOP == 2:
+        pend["a"] = lambda: (agm.finish(), ring_wait(cb, csem, 1))
+    stop(2)
+    ring_wait(cb, csem, 1)
+    go(cb.at[8 - 7 * c], cb.at[9 * c], csem.at[12], csem.at[13], (s, partner))
+    agm.finish()
+    lax.fori_loop(3, 5, wgrad, 0)
     got(cb.at[9 - 9 * c], csem.at[12], csem.at[13])
-    if STOP == 3:
-        pend["a"] = lambda: (ring_wait(csl, xsem, 0), agm.finish())
     stop(3)
 
     def back(i, _):
@@ -545,26 +610,17 @@
     gm[...] = total.astype(BF16)
     to_owner(gm, grecv, gsem)
     pend["gm"] = lambda: owner_wait(grecv, gsem)
-
-    ring_wait(csl, xsem, 0)
-    agm.finish()
+    lax.fori_loop(5, 8, wgrad, 0)
+    if STOP == 8:
+        pend.pop("fz")
+        for q in range(0):
+            pass
+        pend["fz"] = fz
+    stop(8)
+    pend.pop("fz")
+    features_y()
+    pend["part"] = features_wait
     stop(4)
-
-    def wpart(t, ref):
-        ct = jnp.transpose(csl[:, t].reshape(512, 128).astype(F32)).astype(BF16)
-        for a in range(3):
-            wacc[:, 1152 * a : 1152 * a + 1152] += dot(ct, ref[a : a + 8].reshape(512, 1152))
-
-    wpart(s, s2o)
-
-    def wgrad(i, _):
-        t = ((zl + i // 4) % 2) * 4 + (s % 4 + 4 - i % 4) % 4
-        taps10(mk[t], s2)
-        wpart(t, s2)
-        return 0
-
-    lax.fori_loop(1, 8, wgrad, 0)
-    stop(5)
 
     pcp = []
     for q, (lo, n) in enumerate(CHUNKS):
@@ -582,9 +638,9 @@
         ).astype(BF16)
         agw.start(q)
     agw.start_z()
-    if STOP == 6:
+    if STOP == 5:
         agw.rest()
-    stop(6)
+    stop(5)
 
     wait("gm")
     gpf = []
@@ -609,31 +665,21 @@
         t = o[64:128, 128:384] + o[192:256, 256:512] + pltpu.roll(even, 192, 1)
         tbuf[64 * ab : 64 * ab + 64] = (t * SCALE1).astype(BF16)
     tbuf[576:640] = jnp.zeros((64, 256), BF16)
-    lane = pl.ds(pl.multiple_of(c * 128, 128), 128)
-    lane2 = pl.ds(pl.multiple_of(128 - c * 128, 128), 128)
-    k1 = rcopy(tbuf.at[:, lane2], pbuf, ksem.at[0], ksem.at[1], (s, partner))
-    k1.start()
+
+    offs = [(jz, jy, jc) for jz in range(2) for jy in range(4) for jc in range(2) if (jz, jy, jc) != (0, 0, 0)]
+
+    def piece(t):
+        return pl.ds(pl.multiple_of((t // 2) * 80, 16), 80), pl.ds(pl.multiple_of((t % 2) * 128, 128), 128)
+
+    k2s = []
+    for i, o in enumerate(offs):
+        t = depth_peer(d, *o)
+        k2s.append(rcopy(tbuf.at[piece(t)], rbuf.at[i], tsem.at[i], tsem.at[15 + i], (s, t)))
+        k2s[-1].start()
     for q in XF:
         agw.near(q)
-    k1.wait()
-    own[...] = (tbuf[:, lane].astype(F32) + pbuf[...].astype(F32)).astype(BF16)
-    k2s = []
-    for i, (jz, jy) in enumerate(CHIPS):
-        t = depth_peer(d, jz, jy, 0)
-        k2s.append(rcopy(own.at[pl.ds(pl.multiple_of((t // 2) * 80, 16), 80)], rbuf.at[i], tsem.at[i], tsem.at[7 + i], (s, t)))
-        k2s[-1].start()
     for q in ZF:
         agw.across(q)
-    piece = pl.ds(pl.multiple_of(m * 80, 16), 80)
-    tot = own[piece].astype(F32)
-    for i in range(7):
-        k2s[i].wait()
-        tot = tot + rbuf[i].astype(F32)
-    dbuf[7] = tot.astype(BF16)
-    k3s = []
-    for i, (jz, jx) in enumerate(SAMPS):
-        k3s.append(rcopy(dbuf.at[7], dbuf.at[i], tsem.at[14 + i], tsem.at[21 + i], (sample_peer(s, jz, jx), d)))
-        k3s[-1].start()
     if STOP == 7:
         for q in ZF:
             agw.near(q)
@@ -642,30 +688,43 @@
         for q in ZF:
             agw.turn(q)
         agw.finish()
-        for x in k3s:
-            x.wait()
+        pend["k2"] = lambda: [x.wait() for x in k2s]
     stop(7)
+
+    wait("part")
+    tot = frecv[0].astype(F32)
+    for i in range(1, 4):
+        tot = tot + frecv[i].astype(F32)
+    feat[...] = dot(perm64, tot.astype(BF16)).astype(BF16)
 
     wait("ghalo")
     perms = [onehot((32, 32), lambda u, q, b=b: nat(q) == nat(u) + b - 1) for b in range(3)]
     perms[1] = None
     fill_rows(lhsb, edge_planes(gp[...], gpn[...], gn[...], d), perms)
+    tot = tbuf[piece(d)].astype(F32)
+    for i in range(15):
+        k2s[i].wait()
+        tot = tot + rbuf[i].astype(F32)
+    dbuf[7] = tot.astype(BF16)
+    k3s = []
+    for i, (jz, jx) in enumerate(SAMPS):
+        k3s.append(rcopy(dbuf.at[7], dbuf.at[i], tsem.at[30 + i], tsem.at[37 + i], (sample_peer(s, jz, jx), d)))
+        k3s[-1].start()
+    for q in ZF:
+        agw.near(q)
     res = dot(lhsb[...], bandb[...]).astype(BF16)
     wide = jnp.concatenate([res[32 * j : 32 * j + 32] for j in range(8)], axis=1)
     gvol[...] = dot(onehot((32, 32), lambda i, q: nat(q) == i), wide).astype(BF16)
-    for q in ZF:
-        agw.near(q)
     for q in XF:
         agw.far(q)
-
-    wait("part")
-    tot = frecv[0].astype(F32)
-    for i in range(1, 8):
-        tot = tot + frecv[i].astype(F32)
-    feat[...] = dot(perm64, tot.astype(BF16)).astype(BF16)
+    if STOP == 9:
+        for q in ZF:
+            agw.turn(q)
+        agw.finish()
+        pend["k3"] = lambda: [x.wait() for x in k3s]
+    stop(9)
     for q in ZF:
         agw.turn(q)
-
     for x in k3s:
         x.wait()
     tot = None
@@ -674,22 +733,17 @@
         idx = jnp.where(idx == 0, 7, idx - 1)
         val = dbuf[idx].astype(F32)
         tot = val if tot is None else tot + val
-    own[piece] = tot.astype(BF16)
+    tall[piece(d)] = tot.astype(BF16)
     k4s = []
-    for i, (jz, jy) in enumerate(CHIPS):
-        k4s.append(rcopy(own.at[piece], rbuf2.at[i], tsem.at[28 + i], tsem.at[35 + i], (s, depth_peer(d, jz, jy, 0))))
+    for i, o in enumerate(offs):
+        k4s.append(rcopy(tall.at[piece(d)], tall.at[piece(d)], tsem.at[44 + i], tsem.at[59 + i], (s, depth_peer(d, *o))))
         k4s[-1].start()
-    for i, (jz, jy) in enumerate(CHIPS):
-        k4s[i].wait()
-        own[pl.ds(pl.multiple_of((depth_src(d, jz, jy, 0) // 2) * 80, 16), 80)] = rbuf2[i]
-    k5 = rcopy(own, pbuf2, ksem.at[2], ksem.at[3], (s, partner))
-    k5.start()
-    k5.wait()
-    left = jnp.where(c == 0, own[...], pbuf2[...]).astype(F32)
-    right = jnp.where(c == 0, pbuf2[...], own[...]).astype(F32)
+
+    for i, o in enumerate(offs):
+        got(tall.at[piece(depth_src(d, *o))], tsem.at[44 + i], tsem.at[59 + i])
+        k4s[i].wait_send()
     for ab in range(9):
-        both = jnp.concatenate([left[64 * ab : 64 * ab + 64], right[64 * ab : 64 * ab + 64]], axis=1)
-        o1[3 * ab : 3 * ab + 3] = jnp.transpose(both)[0:192].reshape(3, 64, 64)
+        o1[3 * ab : 3 * ab + 3] = jnp.transpose(tall[64 * ab : 64 * ab + 64].astype(F32))[0:192].reshape(3, 64, 64)
     agw.finish()
     for cond, cp in late:
         wait_late(cond, cp)
@@ -702,12 +756,12 @@
     scratch = [
         vm(32, 2048), vm(32, 2048), vm(64, 1024), vm(8, 64, 128), vm(10, 64, 1024), vm(8, 8, 64, 128),
         vm(27, 2, 64, 1024), vm(8, 10, 64, 128), vm(8, 64, 128), vm(256, 4608), vm(256, 4608), vm(4608, 256),
-        vm(4608, 256), vm(10, 64, 1152), vm(10, 64, 1152), vm(8, 64, 1024), vm(8, 64, 1024),
+        vm(4608, 256), vm(10, 64, 1152), vm(10, 64, 1152), vm(8, 64, 1024), vm(8, 64, 1024), vm(4, 64, 1024),
         vm(8, 64, 128), vm(8, 64, 128), vf(9, 512, 128), vf(128, 3456), vf(4, 64, 256), vf(27, 64, 128),
-        vm(27, 64, 128), vm(27, 64, 128), vm(32, 2048), vm(32, 2048), vm(32, 2048), vm(640, 256), vm(640, 128),
-        vm(640, 128), vm(640, 128), vm(7, 80, 128), vm(8, 80, 128), vm(7, 80, 128),
+        vm(27, 64, 128), vm(27, 64, 128), vm(32, 2048), vm(32, 2048), vm(32, 2048), vm(640, 256), vm(640, 256),
+        vm(15, 80, 128), vm(8, 80, 128),
         dma((3,)), dma((8,)), dma((14,)), dma((14,)), dma((14,)), dma((25,)), dma((21,)), dma((21,)), dma((16,)), dma((16,)),
-        dma((14,)), dma((49,)), dma((49,)), dma((4,)), dma((42,)),
+        dma((14,)), dma((49,)), dma((49,)), dma((74,)),
     ]
     return pl.pallas_call(
         mega_kernel,
@@ -720,24 +774,40 @@
     )(v, cot, w1, w)
 
 
-def finish_kernel(gw, t, f, g, o2, o1, of, og):
-    o2[...] = gw[...].astype(F32)
-
-    @pl.when(pl.program_id(0) == 0)
-    def _():
-        of[...] = f[...]
-        og[...] = g[...]
-        o1[...] = t[...]
+def finish_kernel(gw, t, f, g, o2, o1, of, og, narrow, wide, tv, fv, gv, isem, osem):
+    loads = [pltpu.make_async_copy(gw.at[pl.ds(3 * i, 3)], narrow.at[pl.ds(3 * i, 3)], isem.at[i]) for i in range(9)]
+    small_in = [pltpu.make_async_copy(a, b, isem.at[9 + i]) for i, (a, b) in enumerate([(t, tv), (f, fv), (g, gv)])]
+    stores = [pltpu.make_async_copy(wide.at[pl.ds(3 * i, 3)], o2.at[pl.ds(3 * i, 3)], osem.at[i]) for i in range(9)]
+    small_out = [pltpu.make_async_copy(a, b, osem.at[9 + i]) for i, (a, b) in enumerate([(tv, o1), (fv, of), (gv, og)])]
+    for x in loads + small_in:
+        x.start()
+    for i in range(9):
+        loads[i].wait()
+        wide[3 * i : 3 * i + 3] = narrow[3 * i : 3 * i + 3].astype(F32)
+        stores[i].start()
+    for a, b in zip(small_in, small_out):
+        a.wait()
+        b.start()
+    for x in stores + small_out:
+        x.wait()
 
 
 def finish(gw, t, f, g):
-    whole = lambda *shape: pl.BlockSpec(shape, lambda i: (0,) * len(shape))
+    dma = pltpu.SemaphoreType.DMA
     return pl.pallas_call(
         finish_kernel,
-        grid=(9,),
         out_shape=[sds((27, 64, 1024), F32), sds((27, 64, 64), F32), sds((64, 1024)), sds((32, 2048))],
-        in_specs=[pl.BlockSpec((3, 64, 1024), lambda i: (i, 0, 0)), whole(27, 64, 64), whole(64, 1024), whole(32, 2048)],
-        out_specs=[pl.BlockSpec((3, 64, 1024), lambda i: (i, 0, 0)), whole(27, 64, 64), whole(64, 1024), whole(32, 2048)],
+        in_specs=[ANY] * 4,
+        out_specs=[ANY] * 4,
+        scratch_shapes=[
+            pltpu.VMEM((27, 64, 1024), BF16),
+            pltpu.VMEM((27, 64, 1024), F32),
+            pltpu.VMEM((27, 64, 64), F32),
+            pltpu.VMEM((64, 1024), BF16),
+            pltpu.VMEM((32, 2048), BF16),
+            dma((12,)),
+            dma((12,)),
+        ],
         compiler_params=pltpu.CompilerParams(vmem_limit_bytes=LIMIT),
         name="finish",
     )(gw, t, f, g)

time: 104 us -> 99.1 us (0.953)
  Pallas kernels: 103 us -> 98.2 us
    pallas_call x1, Pallas kernels: 8.22 us -> 4.48 us  [finish(): pl.pallas_call(finish_kernel, out_shape=[sds((27, 64, 1024), F32), sds((2...]
    pallas_call x1, Pallas kernels: 94.9 us -> 93.7 us  [mega(): pl.pallas_call(mega_kernel, out_shape=[sds((64, 1024)), sds((32, 2048)),...]
where the time goes in v2:
time: 99.1 us; the launch traced here: 99 us
  Pallas kernels  98.2 us (99%)
    pallas_call x1, Pallas kernels, mega(): pl.pallas_call(mega_kernel, out_shape=[sds((64, 1024)), sds((32, 2048)),...  93.7 us
    pallas_call x1, Pallas kernels, finish(): pl.pallas_call(finish_kernel, out_shape=[sds((27, 64, 1024), F32), sds((2...  4.48 us

profile of v2, /device:TPU:1, one launch (start us, length us, event | category | flops | bytes accessed | tf_op | source)
XLA Modules:
  0.0 99.0 jit_solution(5147320358508381462)
XLA Ops:
  0.6 93.7 %step.1 = (bf16[64,1024]{1,0:T(8,128)(2,1)}, bf16[32,2048]{1,0:T(8,128)(2,1)}, f32[27,64,64]{2,1,0:T(8,128)}, bf16[27,64,1024]{2,1,0:T(8,128)(2,1)}) custom-call(bf16[32,2048]{1,0:T(8,128)(2,1)} %bitcast.4, bf16[64,1024]{1,0:T(8,128)(2,1)} %bitcast.5, bf16[27,64,64]{2,1,0:T(8,128)(2,1)} %refs_2_.1, bf16[27,64,1024]{2,1,0:T(8,128)(2,1)} %refs_3_.1), custom_call_target="tpu_custom_call" | custom-call | tf_op jit(solution)/shard_map/step/pallas_call | solution.py:766
  94.3 4.5 %finish.1 = (f32[27,64,1024]{2,1,0:T(8,128)}, f32[27,64,64]{2,1,0:T(8,128)}, bf16[64,1024]{1,0:T(8,128)(2,1)}, bf16[32,2048]{1,0:T(8,128)(2,1)}) custom-call(bf16[27,64,1024]{2,1,0:T(8,128)(2,1)} %get-tuple-element.12.gw, f32[27,64,64]{2,1,0:T(8,128)} %get-tuple-element.13.t, bf16[64,1024]{1,0:T(8,128)(2,1)} %get-tuple-element.14.f, ...), custom_call_target="tpu_custom_call" | custom-call | tf_op jit(solution)/shard_map/finish/pallas_call | solution.py:797

commit v3 on v2

--- a/solution.py
+++ b/solution.py
@@ -769,7 +769,7 @@
         in_specs=[VM, VM, VM, ANY],
         out_specs=[VM] * 4,
         scratch_shapes=scratch,
-        compiler_params=pltpu.CompilerParams(vmem_limit_bytes=LIMIT, collective_id=1, has_side_effects=True),
+        compiler_params=pltpu.CompilerParams(vmem_limit_bytes=46 * 1024 * 1024, collective_id=1, has_side_effects=True),
         name="step",
     )(v, cot, w1, w)
 
@@ -808,7 +808,7 @@
             dma((12,)),
             dma((12,)),
         ],
-        compiler_params=pltpu.CompilerParams(vmem_limit_bytes=LIMIT),
+        compiler_params=pltpu.CompilerParams(vmem_limit_bytes=16 * 1024 * 1024),
         name="finish",
     )(gw, t, f, g)
 

time: 99.1 us -> 99.8 us (level)
  local copies, waits for them, and re-layouts: 0 us -> 2.81 us
  Pallas kernels: 98.2 us -> 96 us
    pallas_call x1, Pallas kernels: 93.7 us -> 90.3 us  [mega(): pl.pallas_call(mega_kernel, out_shape=[sds((64, 1024)), sds((32, 2048)),...]
    unnamed x0 -> x6, local copies, waits for them, and re-layouts: none -> 2.81 us
    pallas_call x1, Pallas kernels: 4.48 us -> 5.68 us  [finish(): pl.pallas_call(finish_kernel, out_shape=[sds((27, 64, 1024), F32), sds((2...]
where the time goes in v3:
time: 99.8 us; the launch traced here: 99.6 us
  Pallas kernels  96 us (96%)
  local copies, waits for them, and re-layouts  2.81 us (3%)
    pallas_call x1, Pallas kernels, mega(): pl.pallas_call(mega_kernel, out_shape=[sds((64, 1024)), sds((32, 2048)),...  90.3 us
    pallas_call x1, Pallas kernels, finish(): pl.pallas_call(finish_kernel, out_shape=[sds((27, 64, 1024), F32), sds((2...  5.68 us
    unnamed x6, local copies, waits for them, and re-layouts  2.81 us

profile of v3, /device:TPU:1, one launch (start us, length us, event | category | flops | bytes accessed | tf_op | source)
XLA Modules:
  0.0 99.6 jit_solution(1001148105990363285)
XLA Ops:
  0.6 0.0 copy-start
  0.6 1.0 %copy-done = bf16[27,64,64]{2,1,0:T(8,128)(2,1)S(1)} copy-done((bf16[27,64,64]{2,1,0:T(8,128)(2,1)S(1)}, bf16[27,64,64]{2,1,0:T(8,128)(2,1)}, u32[]{:S(2)}) %copy-start) | copy-done | bytes 221208
  1.6 0.0 copy-start.1
  1.6 0.9 copy-done.1
  2.6 0.0 copy-start.2
  2.6 0.9 copy-done.2
  3.5 90.3 %step.1 = (bf16[64,1024]{1,0:T(8,128)(2,1)S(1)}, bf16[32,2048]{1,0:T(8,128)(2,1)S(1)}, f32[27,64,64]{2,1,0:T(8,128)S(1)}, bf16[27,64,1024]{2,1,0:T(8,128)(2,1)S(1)}) custom-call(bf16[32,2048]{1,0:T(8,128)(2,1)S(1)} %bitcast.4, bf16[64,1024]{1,0:T(8,128)(2,1)S(1)} %bitcast.5, bf16[27,64,64]{2,1,0:T(8,128)(2,1)S(1)} %copy-done, bf16[27,64,1024]{2,1,0:T(8,128)(2,1)} %refs_3_.1), custom_call_target="tpu_custom_call" | custom-call | tf_op jit(solution)/shard_map/step/pallas_call | solution.py:766
  93.8 5.7 %finish.1 = (f32[27,64,1024]{2,1,0:T(8,128)}, f32[27,64,64]{2,1,0:T(8,128)}, bf16[64,1024]{1,0:T(8,128)(2,1)}, bf16[32,2048]{1,0:T(8,128)(2,1)}) custom-call(bf16[27,64,1024]{2,1,0:T(8,128)(2,1)S(1)} %get-tuple-element.12.gw, f32[27,64,64]{2,1,0:T(8,128)S(1)} %get-tuple-element.13.t, bf16[64,1024]{1,0:T(8,128)(2,1)S(1)} %get-tuple-element.14.f, ...), custom_call_target="tpu_custom_call" | custom-call | tf_op jit(solution)/shard_map/finish/pallas_call | solution.py:797
Async XLA Ops:
  0.6 1.0 %copy-start = (bf16[27,64,64]{2,1,0:T(8,128)(2,1)S(1)}, bf16[27,64,64]{2,1,0:T(8,128)(2,1)}, u32[]{:S(2)}) copy-start(bf16[27,64,64]{2,1,0:T(8,128)(2,1)} %refs_2_.1) | copy-start | bytes 663556
  1.6 0.9 copy-start.1
  2.6 0.9 copy-start.2

commit v4 on v2

--- a/solution.py
+++ b/solution.py
@@ -177,8 +177,8 @@
 
 
 CHUNKS = [(4 * q, min(4, 27 - 4 * q)) for q in range(7)]
-XF = (0, 1, 2)
-ZF = (3, 4, 5, 6)
+XF = (0, 1)
+ZF = (2, 3, 4, 5, 6)
 
 
 def mega_kernel(*refs):
@@ -611,15 +611,6 @@
     to_owner(gm, grecv, gsem)
     pend["gm"] = lambda: owner_wait(grecv, gsem)
     lax.fori_loop(5, 8, wgrad, 0)
-    if STOP == 8:
-        pend.pop("fz")
-        for q in range(0):
-            pass
-        pend["fz"] = fz
-    stop(8)
-    pend.pop("fz")
-    features_y()
-    pend["part"] = features_wait
     stop(4)
 
     pcp = []
@@ -676,6 +667,15 @@
         t = depth_peer(d, *o)
         k2s.append(rcopy(tbuf.at[piece(t)], rbuf.at[i], tsem.at[i], tsem.at[15 + i], (s, t)))
         k2s[-1].start()
+    if STOP == 8:
+        pend.pop("fz")
+        for q in range(0):
+            pass
+        pend["fz"] = fz
+    stop(8)
+    pend.pop("fz")
+    features_y()
+    pend["part"] = features_wait
     for q in XF:
         agw.near(q)
     for q in ZF:
@@ -690,12 +690,6 @@
         agw.finish()
         pend["k2"] = lambda: [x.wait() for x in k2s]
     stop(7)
-
-    wait("part")
-    tot = frecv[0].astype(F32)
-    for i in range(1, 4):
-        tot = tot + frecv[i].astype(F32)
-    feat[...] = dot(perm64, tot.astype(BF16)).astype(BF16)
 
     wait("ghalo")
     perms = [onehot((32, 32), lambda u, q, b=b: nat(q) == nat(u) + b - 1) for b in range(3)]
@@ -723,6 +717,12 @@
         agw.finish()
         pend["k3"] = lambda: [x.wait() for x in k3s]
     stop(9)
+    wait("part")
+    tot = frecv[0].astype(F32)
+    for i in range(1, 4):
+        tot = tot + frecv[i].astype(F32)
+    feat[...] = dot(perm64, tot.astype(BF16)).astype(BF16)
+
     for q in ZF:
         agw.turn(q)
     for x in k3s:

time: 99.1 us -> 95.3 us (0.962)
  Pallas kernels: 98.2 us -> 94.4 us
    pallas_call x1, Pallas kernels: 93.7 us -> 89.9 us  [mega(): pl.pallas_call(mega_kernel, out_shape=[sds((64, 1024)), sds((32, 2048)),...]
where the time goes in v4:
time: 95.3 us; the launch traced here: 95.2 us
  Pallas kernels  94.4 us (99%)
    pallas_call x1, Pallas kernels, mega(): pl.pallas_call(mega_kernel, out_shape=[sds((64, 1024)), sds((32, 2048)),...  89.9 us
    pallas_call x1, Pallas kernels, finish(): pl.pallas_call(finish_kernel, out_shape=[sds((27, 64, 1024), F32), sds((2...  4.48 us

profile of v4, /device:TPU:1, one launch (start us, length us, event | category | flops | bytes accessed | tf_op | source)
XLA Modules:
  0.0 95.2 jit_solution(16554845620159973642)
XLA Ops:
  0.6 89.9 %step.1 = (bf16[64,1024]{1,0:T(8,128)(2,1)}, bf16[32,2048]{1,0:T(8,128)(2,1)}, f32[27,64,64]{2,1,0:T(8,128)}, bf16[27,64,1024]{2,1,0:T(8,128)(2,1)}) custom-call(bf16[32,2048]{1,0:T(8,128)(2,1)} %bitcast.4, bf16[64,1024]{1,0:T(8,128)(2,1)} %bitcast.5, bf16[27,64,64]{2,1,0:T(8,128)(2,1)} %refs_2_.1, bf16[27,64,1024]{2,1,0:T(8,128)(2,1)} %refs_3_.1), custom_call_target="tpu_custom_call" | custom-call | tf_op jit(solution)/shard_map/step/pallas_call | solution.py:766
  90.5 4.5 %finish.1 = (f32[27,64,1024]{2,1,0:T(8,128)}, f32[27,64,64]{2,1,0:T(8,128)}, bf16[64,1024]{1,0:T(8,128)(2,1)}, bf16[32,2048]{1,0:T(8,128)(2,1)}) custom-call(bf16[27,64,1024]{2,1,0:T(8,128)(2,1)} %get-tuple-element.12.gw, f32[27,64,64]{2,1,0:T(8,128)} %get-tuple-element.13.t, bf16[64,1024]{1,0:T(8,128)(2,1)} %get-tuple-element.14.f, ...), custom_call_target="tpu_custom_call" | custom-call | tf_op jit(solution)/shard_map/finish/pallas_call | solution.py:797
